TPU v7x, 256 devices: a whole 4x4x8 slice. The times are simulated.
256 devices in a mesh: wide: 32 (over y, x, core), narrow: 8 (over z).
Axes of the slice: x: 4, y: 4, z: 8, core: 2. Of those that a mesh axis runs over, the one named last changes fastest.
Arguments:
- features: bfloat16 [1024, 16384], P('wide', 'narrow'), may hold values from -6 to 6
- queries: bfloat16 [2048, 16384], P('wide', 'narrow'), may hold values from -6 to 6
- damping: float32 [16384], P('wide'), may hold values from 0.25 to 4
Outputs:
- kernel: float32 [16384, 16384], P('wide', 'narrow')
- factor: float32 [16384, 256], P('wide')
- scores: float32 [2048, 1024], P('wide', 'narrow')
All inputs are finite; a program needn't handle non-finite values.
Results may differ from a plain program's by a relative error of at most 0.0003.
Values may be sent and summed in bfloat16 or wider, within the bound.
A program may use at most 64 MiB of HBM per device.

v0:
```python
import math
import jax
import jax.numpy as jnp
from jax import lax
from jax.sharding import PartitionSpec as P

P_SIZE = 16384
PANEL = 128
PANELS = 2


def laid_out(pieces, dim):
    pieces = jnp.moveaxis(pieces, 0, dim)
    shape = pieces.shape
    return pieces.reshape(*shape[:dim], shape[dim] * shape[dim + 1], *shape[dim + 2 :])


def copy_for_each(x, axis):
    copies = jnp.broadcast_to(x, (lax.axis_size(axis), *x.shape))
    return lax.all_to_all(copies, axis, split_axis=0, concat_axis=0, tiled=True)


def collect(x, axis, dim):
    return laid_out(copy_for_each(x, axis), dim)


def in_blocks(x, dim, size):
    before, after = (x.shape[:dim], x.shape[dim + 1 :])
    return jnp.moveaxis(x.reshape(*before, size, -1, *after), dim, 0)


def sent_and_summed(x, axis, dim):
    size = lax.axis_size(axis)
    pieces = lax.all_to_all(in_blocks(x, dim, size), axis, 0, 0, tiled=True)
    return jnp.sum(pieces, axis=0)


def broadcast(x, axis, root):
    return lax.dynamic_index_in_dim(lax.all_gather(x, axis), root, 0, keepdims=False)


def on_device(features, queries, damping):
    rows_here = damping.shape[0]
    cols_here = queries.shape[1]
    slab_total = features.shape[0] * lax.axis_size("wide")
    wide_pos = lax.axis_index("wide")
    narrow_pos = lax.axis_index("narrow")
    contract_rows = (((0,), (0,)), ((), ()))
    contract_cols = (((1,), (1,)), ((), ()))
    full_width = collect(features, "narrow", 1)
    row_features = lax.all_to_all(full_width, "wide", split_axis=1, concat_axis=0, tiled=True)
    slab_columns = lax.all_gather(features, "wide", axis=0, tiled=True)
    products = lax.dot_general(
        row_features, slab_columns, contract_rows, preferred_element_type=jnp.float32
    )
    partial_value = lax.dot_general(
        queries, slab_columns, contract_cols, preferred_element_type=jnp.float32
    )
    scores = sent_and_summed(partial_value, "narrow", 1) * (1.0 / math.sqrt(P_SIZE))
    row_ids = wide_pos * rows_here + lax.broadcasted_iota(jnp.int32, (rows_here, 1), 0)
    col_ids = narrow_pos * cols_here + lax.broadcasted_iota(jnp.int32, (1, cols_here), 1)
    kernel_block = products / slab_total + jnp.where(
        row_ids == col_ids, damping[:, None], jnp.float32(0.0)
    )
    factors = []
    for panel_index in range(PANELS):
        offset = panel_index * PANEL
        column_root = offset // cols_here
        row_root = offset // rows_here
        col_shift = offset % cols_here
        row_shift = offset % rows_here
        panel_columns = broadcast(
            kernel_block[:, col_shift : col_shift + PANEL], "narrow", column_root
        )
        pivot_block = broadcast(panel_columns[row_shift : row_shift + PANEL], "wide", row_root)
        pivot_factor = jnp.linalg.cholesky(pivot_block)
        lower_rows = lax.linalg.triangular_solve(
            pivot_factor, panel_columns, left_side=False, lower=True, transpose_a=True
        )
        per_group = cols_here // rows_here
        pieces = []
        for member in range(per_group):
            pieces.append(broadcast(lower_rows, "wide", narrow_pos * per_group + member))
        lower_cols = jnp.concatenate(pieces, axis=0)
        kernel_block = kernel_block - jnp.dot(
            lower_rows,
            lower_cols.T,
            precision=lax.Precision.HIGHEST,
            preferred_element_type=jnp.float32,
        )
        boundary = offset + PANEL
        kernel_block = jnp.where(
            (row_ids < boundary) | (col_ids < boundary), jnp.zeros_like(kernel_block), kernel_block
        )
        factors.append(lower_rows)
    return (kernel_block, jnp.concatenate(factors, axis=1), scores)


def solution(mesh):
    return jax.shard_map(
        on_device,
        mesh=mesh,
        in_specs=(P("wide", "narrow"), P("wide", "narrow"), P("wide")),
        out_specs=(P("wide", "narrow"), P("wide", None), P("wide", "narrow")),
        check_vma=False,
    )
```

profile of v0, /device:TPU:1, one launch (start us, length us, event | category | flops | bytes accessed | tf_op | source)
XLA Modules:
  0.0 475.1 jit_solution(2787711246564530403)
XLA Ops:
  8.9 36.2 %all_to_all.29 = bf16[8,32,2048]{2,1,0:T(8,128)(2,1)S(1)} all-to-all(bf16[8,32,2048]{2,1,0:T(8,128)(2,1)S(1)} %broadcast_in_dim.15), channel_id=1, replica_groups=mesh['wide'=32,'narrow'=8] {'narrow'}, dimensions={0} | all-to-all | bytes 2097152 | tf_op jit(solution)/shard_map/all_to_all | solution.py:20
  47.9 9.4 %all-to-all-start.1 = ((bf16[32,32,512]{2,0,1:T(8,128)(2,1)}), bf16[32,32,512]{2,0,1:T(8,128)(2,1)S(1)}, u32[]{:S(2)}, u32[]{:S(2)}) async-start(bf16[32,32,512]{2,0,1:T(8,128)(2,1)} %copy.16), calls=%async_computation.1 | async-start | bytes 2097152 | tf_op jit(solution)/shard_map/all_to_all | solution.py:51
  57.4 18.8 %all-to-all-done.1 = bf16[32,32,512]{2,0,1:T(8,128)(2,1)S(1)} async-done(((bf16[32,32,512]{2,0,1:T(8,128)(2,1)}), bf16[32,32,512]{2,0,1:T(8,128)(2,1)S(1)}, u32[]{:S(2)}, u32[]{:S(2)}) %all-to-all-start.1) | async-done | bytes 1048608 | tf_op jit(solution)/shard_map/all_to_all | solution.py:51
  76.2 5.0 %select_add_fusion = f32[512,2048]{1,0:T(8,128)S(1)} fusion(bf16[1024,512]{1,0:T(8,128)(2,1)S(1)} %bitcast.87, bf16[1024,2048]{1,0:T(8,128)(2,1)} %all-gather.12.cloned.1.call-done, f32[512]{0:T(512)S(1)} %copy-done.7, s32[2048]{0:T(1024)S(1)} %iota_add_fusion, s32[512]{0:T(512)S(1)} %iota_add_fusion.1), kind=kOutput, calls=%fused_computation.2 | convolution fusion | flops 2151677952 | bytes 9449472 | tf_op jit(solution)/shard_map/dot_general | solution.py:53
  81.2 2.0 copy-done.3
  84.0 33.5 %all-gather.18.cloned.1.call-done = f32[4096,128]{1,0:T(8,128)} async-done(((f32[512,128]{1,0:T(8,128)}), f32[4096,128]{1,0:T(8,128)}) %all-gather.18.cloned.1.call-update) | async-done | bytes 2097168 | tf_op jit(solution)/shard_map/all_gather | solution.py:39
  119.1 53.3 %all-gather.14.cloned.1.call-done = f32[32,128,128]{2,1,0:T(8,128)} async-done(((f32[1,128,128]{2,1,0:T(8,128)}), f32[32,128,128]{2,1,0:T(8,128)}) %all-gather.14.cloned.1.call-update) | async-done | bytes 2097168 | tf_op jit(solution)/shard_map/all_gather | solution.py:39
  174.2 11.7 %cholesky.44 = f32[128,128]{1,0:T(8,128)S(1)} custom-call(f32[128,128]{1,0:T(8,128)S(1)} %fusion.19), custom_call_target="Cholesky" | custom-call | tf_op jit(solution)/shard_map/jit(cholesky)/cholesky | solution.py:76
  187.3 9.8 %custom-call.6 = f32[1,128,128]{1,2,0:T(8,128)S(1)} custom-call(f32[1,128,128]{2,1,0:T(8,128)S(1)} %fusion.16), custom_call_target="InvertDiagBlocksLowerTriangular" | custom-call | tf_op jit(solution)/shard_map/triangular_solve/custom-call.0 | solution.py:77
  197.1 2.1 convolution_bitcast_fusion.2
  199.8 56.8 %all-gather.20.cloned.1.call-done = f32[16384,128]{0,1:T(8,128)} async-done(((f32[512,128]{0,1:T(8,128)}), f32[16384,128]{0,1:T(8,128)}) %all-gather.20.cloned.1.call-update) | async-done | bytes 8388624 | tf_op jit(solution)/shard_map/all_gather | solution.py:39
  256.6 9.9 %copy.36 = f32[16,8,32,512]{3,2,1,0:T(8,128)S(1)} copy(f32[16,8,32,512]{3,1,2,0:T(8,128)} %bitcast.80) | data formatting | bytes 16777216
  268.7 4.1 subtract_select_fusion.1
  275.6 36.0 %all-gather.22.cloned.1.call-done = f32[4096,128]{1,0:T(8,128)} async-done(((f32[512,128]{1,0:T(8,128)}), f32[4096,128]{1,0:T(8,128)}) %all-gather.22.cloned.1.call-update) | async-done | bytes 2097168 | tf_op jit(solution)/shard_map/all_gather | solution.py:39
  313.3 53.0 %all-gather.16.cloned.1.call-done = f32[32,128,128]{2,1,0:T(8,128)} async-done(((f32[1,128,128]{2,1,0:T(8,128)}), f32[32,128,128]{2,1,0:T(8,128)}) %all-gather.16.cloned.1.call-update) | async-done | bytes 2097168 | tf_op jit(solution)/shard_map/all_gather | solution.py:39
  368.1 11.7 %cholesky.55 = f32[128,128]{1,0:T(8,128)S(1)} custom-call(f32[128,128]{1,0:T(8,128)S(1)} %fusion.18), custom_call_target="Cholesky" | custom-call | tf_op jit(solution)/shard_map/jit(cholesky)/cholesky | solution.py:76
  381.2 9.8 %custom-call.7 = f32[1,128,128]{1,2,0:T(8,128)S(1)} custom-call(f32[1,128,128]{2,1,0:T(8,128)S(1)} %fusion.17), custom_call_target="InvertDiagBlocksLowerTriangular" | custom-call | tf_op jit(solution)/shard_map/triangular_solve/custom-call.0 | solution.py:77
  391.0 2.1 convolution_bitcast_fusion.1
  393.1 3.6 convolution_bitcast_fusion
  397.5 7.0 %all-to-all-start.2 = ((f32[8,64,128]{2,1,0:T(8,128)}), f32[8,64,128]{2,1,0:T(8,128)S(1)}, u32[]{:S(2)}, u32[]{:S(2)}) async-start(f32[8,64,128]{2,1,0:T(8,128)} %bitcast.73), calls=%async_computation.2 | async-start | bytes 524288 | tf_op jit(solution)/shard_map/all_to_all | solution.py:34
  404.5 11.6 %all-to-all-done.2 = f32[8,64,128]{2,1,0:T(8,128)S(1)} async-done(((f32[8,64,128]{2,1,0:T(8,128)}), f32[8,64,128]{2,1,0:T(8,128)S(1)}, u32[]{:S(2)}, u32[]{:S(2)}) %all-to-all-start.2) | async-done | bytes 262176 | tf_op jit(solution)/shard_map/all_to_all | solution.py:34
  417.8 32.7 %all-gather.24.cloned.1.call-done = f32[16384,128]{0,1:T(8,128)} async-done(((f32[512,128]{0,1:T(8,128)}), f32[16384,128]{0,1:T(8,128)}) %all-gather.24.cloned.1.call-update) | async-done | bytes 8388624 | tf_op jit(solution)/shard_map/all_gather | solution.py:39
  450.5 9.9 %copy.37 = f32[16,8,32,512]{3,2,1,0:T(8,128)S(1)} copy(f32[16,8,32,512]{3,1,2,0:T(8,128)} %bitcast.81) | data formatting | bytes 16777216
  462.6 5.5 %subtract_select_fusion = f32[512,2048]{1,0:T(8,128)} fusion(f32[512,2048]{1,0:T(8,128)S(1)} %copy-done.2, f32[512,128]{0,1:T(8,128)S(1)} %copy-done.6, pred[2048]{0:T(1024)(128)(4,1)S(1)} %fusion.23, pred[512]{0:T(512)(128)(4,1)S(1)} %fusion.25, f32[512,128]{0,1:T(8,128)S(1)} %bitcast.84, f32[512,128]{0,1:T(8,128)S(1)} %bitcast.85, ...), kind=kOutput, calls=%fused_computation | convolution fusion | flops 1614544896 | bytes 9701888 | tf_op jit(solution)/shard_map/dot_general | solution.py:85
  (69 shorter events, 24.9 us)
Async XLA Ops:
  7.2 386.0 %copy-start = (bf16[64,2048]{1,0:T(8,128)(2,1)S(1)}, bf16[64,2048]{1,0:T(8,128)(2,1)}, u32[]{:S(2)}) copy-start(bf16[64,2048]{1,0:T(8,128)(2,1)} %param.7) | copy-start | bytes 786436
  7.2 69.1 %all-gather.12.cloned.1.call-start = ((), (), s32[]{:S(2)}) async-start(), calls=%async_computation.3 | async-start | bytes 4325376 | tf_op jit(solution)/shard_map/all_gather | solution.py:52
  45.1 31.2 %copy-start.7 = (f32[512]{0:T(512)S(1)}, f32[512]{0:T(512)}, u32[]{:S(2)}) copy-start(f32[512]{0:T(512)} %param.8) | copy-start | bytes 6148
  47.9 28.3 %all-to-all-start.1 = ((bf16[32,32,512]{2,0,1:T(8,128)(2,1)}), bf16[32,32,512]{2,0,1:T(8,128)(2,1)S(1)}, u32[]{:S(2)}, u32[]{:S(2)}) async-start(bf16[32,32,512]{2,0,1:T(8,128)(2,1)} %copy.16), calls=%async_computation.1 | async-start | bytes 2097152 | tf_op jit(solution)/shard_map/all_to_all | solution.py:51
  57.3 60.2 %all-gather.18.cloned.1.call-start = ((), (), s32[]{:S(2)}) async-start(), calls=%async_computation.6 | async-start | bytes 2359296 | tf_op jit(solution)/shard_map/all_gather | solution.py:39
  81.2 2.0 copy-start.3
  84.0 88.5 %all-gather.14.cloned.1.call-start = ((), (), s32[]{:S(2)}) async-start(), calls=%async_computation.4 | async-start | bytes 2162688 | tf_op jit(solution)/shard_map/all_gather | solution.py:39
  119.1 137.5 %all-gather.20.cloned.1.call-start = ((), (), s32[]{:S(2)}) async-start(), calls=%async_computation.7 | async-start | bytes 8650752 | tf_op jit(solution)/shard_map/all_gather | solution.py:39
  199.2 112.4 %all-gather.22.cloned.1.call-start = ((), (), s32[]{:S(2)}) async-start(), calls=%async_computation.8 | async-start | bytes 2359296 | tf_op jit(solution)/shard_map/all_gather | solution.py:39
  256.6 11.2 %copy-start.5 = (f32[512,128]{0,1:T(8,128)S(1)}, f32[512,128]{0,1:T(8,128)}, u32[]{:S(2)}) copy-start(f32[512,128]{0,1:T(8,128)} %convolution_bitcast_fusion.2) | copy-start | bytes 786436
  266.5 2.2 copy-start.4
  272.8 2.0 copy-start.1
  275.5 90.8 %all-gather.16.cloned.1.call-start = ((), (), s32[]{:S(2)}) async-start(), calls=%async_computation.5 | async-start | bytes 2162688 | tf_op jit(solution)/shard_map/all_gather | solution.py:39
  313.1 137.4 %all-gather.24.cloned.1.call-start = ((), (), s32[]{:S(2)}) async-start(), calls=%async_computation.9 | async-start | bytes 8650752 | tf_op jit(solution)/shard_map/all_gather | solution.py:39
  393.1 23.7 %copy-start.6 = (f32[512,128]{0,1:T(8,128)S(1)}, f32[512,128]{0,1:T(8,128)}, u32[]{:S(2)}) copy-start(f32[512,128]{0,1:T(8,128)} %convolution_bitcast_fusion.1) | copy-start | bytes 786436
  397.5 18.6 %all-to-all-start.2 = ((f32[8,64,128]{2,1,0:T(8,128)}), f32[8,64,128]{2,1,0:T(8,128)S(1)}, u32[]{:S(2)}, u32[]{:S(2)}) async-start(f32[8,64,128]{2,1,0:T(8,128)} %bitcast.73), calls=%async_computation.2 | async-start | bytes 524288 | tf_op jit(solution)/shard_map/all_to_all | solution.py:34
  460.4 2.2 copy-start.2
Sparse Core Ops, SparseCore 0:
  10.5 60.5 all-gather.11
  84.1 33.4 all-gather.17
  120.7 51.7 all-gather.13
  199.3 57.1 all-gather.19
  275.7 35.8 all-gather.21
  314.6 51.7 all-gather.15
  393.3 57.1 all-gather.23
where the time goes:
time: 484 us; the launch traced here: 475 us
  waiting for transfers between devices  297 us (61%)
  other arithmetic  48.1 us (10%)
  local copies, waits for them, and re-layouts  39.9 us (8%)
  blocking collectives  36.2 us (7%)
  matrix products  22.3 us (5%)
  starting transfers between devices  17.3 us (4%)
  between operations  14.6 us (3%)
    all_gather x6, waiting for transfers between devices, broadcast(): lax.all_gather(x, axis)  265 us
    all_to_all x1, blocking collectives, copy_for_each(): return lax.all_to_all(copies, axis, split_axis=0, concat_axis=0, tiled=True)  36.2 us
    unnamed x27, local copies, waits for them, and re-layouts  26.9 us
    another operation x6, other arithmetic, on_device(): pivot_factor = jnp.linalg.cholesky(pivot_block)  24.8 us
    another operation x4, other arithmetic, on_device(): lax.linalg.triangular_solve(pivot_factor, panel_columns, left_side=False,...  20.9 us
    all_to_all x1, waiting for transfers between devices, on_device(): lax.all_to_all(full_width, 'wide', split_axis=1, concat_axis=0, tiled=True)  18.8 us
    all_to_all x1, waiting for transfers between devices, sent_and_summed(): pieces = lax.all_to_all(in_blocks(x, dim, size), axis, 0, 0, tiled=True)  11.6 us
  transfers between devices with their start and end apart: 9, of which 8 were waited for; matrix products, arithmetic and copies ran while one was open for 2% of the time, Pallas kernels for 0%

commit v1 on v0

--- a/solution.py
+++ b/solution.py
@@ -48,7 +48,12 @@
     contract_rows = (((0,), (0,)), ((), ()))
     contract_cols = (((1,), (1,)), ((), ()))
     full_width = collect(features, "narrow", 1)
-    row_features = lax.all_to_all(full_width, "wide", split_axis=1, concat_axis=0, tiled=True)
+    row_features = jnp.concatenate(
+        lax.all_to_all(
+            jnp.stack(jnp.split(full_width, lax.axis_size("wide"), axis=1)), "wide", 0, 0
+        ),
+        axis=0,
+    )
     slab_columns = lax.all_gather(features, "wide", axis=0, tiled=True)
     products = lax.dot_general(
         row_features, slab_columns, contract_rows, preferred_element_type=jnp.float32

time: 484 us -> 495 us (1.023)
  blocking collectives: 36.2 us -> 0 us
  waiting for transfers between devices: 297 us -> 319 us
  local copies, waits for them, and re-layouts: 39.9 us -> 58 us
  starting transfers between devices: 17.3 us -> 24.6 us
    all_to_all x1 -> x0, blocking collectives: 36.2 us -> none  [copy_for_each(): return lax.all_to_all(copies, axis, split_axis=0, concat_axis=0, tiled=True)]
    all_to_all x1 -> x2, waiting for transfers between devices: 18.8 us -> 45.4 us  [the longest x1 28.5 us: copy_for_each(): return lax.all_to_all(copies, axis, split_axis=0, concat_axis=0, tiled=True)]
    unnamed x27 -> x58, local copies, waits for them, and re-layouts: 26.9 us -> 46.1 us
    all_to_all x1 -> x2, starting transfers between devices: 9.42 us -> 16.7 us  [the longest x1 9.13 us: copy_for_each(): return lax.all_to_all(copies, axis, split_axis=0, concat_axis=0, tiled=True)]
  transfers between devices with their start and end apart: 9 -> 10, of which waited for: 8 -> 9; matrix products, arithmetic and copies ran while one was open for 2% -> 5% of each run, Pallas kernels for 0% -> 0%
where the time goes in v1:
time: 495 us; the launch traced here: 487 us
  waiting for transfers between devices  319 us (64%)
  local copies, waits for them, and re-layouts  58 us (12%)
  other arithmetic  48.1 us (10%)
  starting transfers between devices  24.6 us (5%)
  matrix products  22.3 us (5%)
  between operations  14.7 us (3%)
    all_gather x6, waiting for transfers between devices, broadcast(): lax.all_gather(x, axis)  261 us
    unnamed x58, local copies, waits for them, and re-layouts  46.1 us
    all_to_all x1, waiting for transfers between devices, copy_for_each(): return lax.all_to_all(copies, axis, split_axis=0, concat_axis=0, tiled=True)  28.5 us
    another operation x6, other arithmetic, on_device(): pivot_factor = jnp.linalg.cholesky(pivot_block)  24.8 us
    another operation x4, other arithmetic, on_device(): lax.linalg.triangular_solve(pivot_factor, panel_columns, left_side=False,...  20.9 us
    all_to_all x1, waiting for transfers between devices, on_device(): lax.all_to_all(jnp.stack(jnp.split(full_width, lax.axis_size('wide'), axi...  17 us
    all_to_all x1, waiting for transfers between devices, sent_and_summed(): pieces = lax.all_to_all(in_blocks(x, dim, size), axis, 0, 0, tiled=True)  11.6 us
  transfers between devices with their start and end apart: 10, of which 9 were waited for; matrix products, arithmetic and copies ran while one was open for 5% of the time, Pallas kernels for 0%

profile of v1, /device:TPU:1, one launch (start us, length us, event | category | flops | bytes accessed | tf_op | source)
XLA Modules:
  0.0 486.7 jit_solution(17475636749044794800)
XLA Ops:
  9.2 9.1 %all-to-all-start = ((bf16[8,32,2048]{2,1,0:T(8,128)(2,1)}), bf16[8,32,2048]{2,1,0:T(8,128)(2,1)S(1)}, u32[]{:S(2)}, u32[]{:S(2)}) async-start(bf16[8,32,2048]{2,1,0:T(8,128)(2,1)} %broadcast_in_dim.15), calls=%async_computation | async-start | bytes 2097152 | tf_op jit(solution)/shard_map/all_to_all | solution.py:20
  19.1 28.5 %all-to-all-done = bf16[8,32,2048]{2,1,0:T(8,128)(2,1)S(1)} async-done(((bf16[8,32,2048]{2,1,0:T(8,128)(2,1)}), bf16[8,32,2048]{2,1,0:T(8,128)(2,1)S(1)}, u32[]{:S(2)}, u32[]{:S(2)}) %all-to-all-start) | async-done | bytes 1048608 | tf_op jit(solution)/shard_map/all_to_all | solution.py:20
  67.4 7.6 %all-to-all-start.1 = ((bf16[32,32,512]{2,1,0:T(8,128)(2,1)}), bf16[32,32,512]{2,1,0:T(8,128)(2,1)S(1)}, u32[]{:S(2)}, u32[]{:S(2)}) async-start(bf16[32,32,512]{2,1,0:T(8,128)(2,1)} %constant_dynamic-update-slice_fusion), calls=%async_computation.1 | async-start | bytes 2097152 | tf_op jit(solution)/shard_map/all_to_all | solution.py:52
  75.1 17.0 %all-to-all-done.1 = bf16[32,32,512]{2,1,0:T(8,128)(2,1)S(1)} async-done(((bf16[32,32,512]{2,1,0:T(8,128)(2,1)}), bf16[32,32,512]{2,1,0:T(8,128)(2,1)S(1)}, u32[]{:S(2)}, u32[]{:S(2)}) %all-to-all-start.1) | async-done | bytes 1048608 | tf_op jit(solution)/shard_map/all_to_all | solution.py:52
  92.0 5.0 %select_add_fusion = f32[512,2048]{1,0:T(8,128)S(1)} fusion(bf16[1024,512]{1,0:T(8,128)(2,1)S(1)} %bitcast.247, bf16[1024,2048]{1,0:T(8,128)(2,1)} %all-gather.12.cloned.1.call-done, f32[512]{0:T(512)S(1)} %copy-done.7, s32[2048]{0:T(1024)S(1)} %iota_add_fusion, s32[512]{0:T(512)S(1)} %iota_add_fusion.1), kind=kOutput, calls=%fused_computation.2 | convolution fusion | flops 2151677952 | bytes 9449472 | tf_op jit(solution)/shard_map/dot_general | solution.py:58
  99.8 29.3 %all-gather.18.cloned.1.call-done = f32[4096,128]{1,0:T(8,128)} async-done(((f32[512,128]{1,0:T(8,128)}), f32[4096,128]{1,0:T(8,128)}) %all-gather.18.cloned.1.call-update) | async-done | bytes 2097168 | tf_op jit(solution)/shard_map/all_gather | solution.py:39
  130.7 53.3 %all-gather.14.cloned.1.call-done = f32[32,128,128]{2,1,0:T(8,128)} async-done(((f32[1,128,128]{2,1,0:T(8,128)}), f32[32,128,128]{2,1,0:T(8,128)}) %all-gather.14.cloned.1.call-update) | async-done | bytes 2097168 | tf_op jit(solution)/shard_map/all_gather | solution.py:39
  185.9 11.7 %cholesky.44 = f32[128,128]{1,0:T(8,128)S(1)} custom-call(f32[128,128]{1,0:T(8,128)S(1)} %fusion.19), custom_call_target="Cholesky" | custom-call | tf_op jit(solution)/shard_map/jit(cholesky)/cholesky | solution.py:81
  198.9 9.8 %custom-call.6 = f32[1,128,128]{1,2,0:T(8,128)S(1)} custom-call(f32[1,128,128]{2,1,0:T(8,128)S(1)} %fusion.16), custom_call_target="InvertDiagBlocksLowerTriangular" | custom-call | tf_op jit(solution)/shard_map/triangular_solve/custom-call.0 | solution.py:82
  208.7 2.1 convolution_bitcast_fusion.2
  211.4 56.8 %all-gather.20.cloned.1.call-done = f32[16384,128]{0,1:T(8,128)} async-done(((f32[512,128]{0,1:T(8,128)}), f32[16384,128]{0,1:T(8,128)}) %all-gather.20.cloned.1.call-update) | async-done | bytes 8388624 | tf_op jit(solution)/shard_map/all_gather | solution.py:39
  268.2 9.9 %copy.35 = f32[16,8,32,512]{3,2,1,0:T(8,128)S(1)} copy(f32[16,8,32,512]{3,1,2,0:T(8,128)} %bitcast.208) | data formatting | bytes 16777216
  280.3 4.1 subtract_select_fusion.1
  287.2 36.0 %all-gather.22.cloned.1.call-done = f32[4096,128]{1,0:T(8,128)} async-done(((f32[512,128]{1,0:T(8,128)}), f32[4096,128]{1,0:T(8,128)}) %all-gather.22.cloned.1.call-update) | async-done | bytes 2097168 | tf_op jit(solution)/shard_map/all_gather | solution.py:39
  324.9 53.0 %all-gather.16.cloned.1.call-done = f32[32,128,128]{2,1,0:T(8,128)} async-done(((f32[1,128,128]{2,1,0:T(8,128)}), f32[32,128,128]{2,1,0:T(8,128)}) %all-gather.16.cloned.1.call-update) | async-done | bytes 2097168 | tf_op jit(solution)/shard_map/all_gather | solution.py:39
  379.8 11.7 %cholesky.55 = f32[128,128]{1,0:T(8,128)S(1)} custom-call(f32[128,128]{1,0:T(8,128)S(1)} %fusion.18), custom_call_target="Cholesky" | custom-call | tf_op jit(solution)/shard_map/jit(cholesky)/cholesky | solution.py:81
  392.8 9.8 %custom-call.7 = f32[1,128,128]{1,2,0:T(8,128)S(1)} custom-call(f32[1,128,128]{2,1,0:T(8,128)S(1)} %fusion.17), custom_call_target="InvertDiagBlocksLowerTriangular" | custom-call | tf_op jit(solution)/shard_map/triangular_solve/custom-call.0 | solution.py:82
  402.6 2.1 convolution_bitcast_fusion.1
  404.8 3.6 convolution_bitcast_fusion
  409.1 7.0 %all-to-all-start.2 = ((f32[8,64,128]{2,1,0:T(8,128)}), f32[8,64,128]{2,1,0:T(8,128)S(1)}, u32[]{:S(2)}, u32[]{:S(2)}) async-start(f32[8,64,128]{2,1,0:T(8,128)} %bitcast.201), calls=%async_computation.2 | async-start | bytes 524288 | tf_op jit(solution)/shard_map/all_to_all | solution.py:34
  416.1 11.6 %all-to-all-done.2 = f32[8,64,128]{2,1,0:T(8,128)S(1)} async-done(((f32[8,64,128]{2,1,0:T(8,128)}), f32[8,64,128]{2,1,0:T(8,128)S(1)}, u32[]{:S(2)}, u32[]{:S(2)}) %all-to-all-start.2) | async-done | bytes 262176 | tf_op jit(solution)/shard_map/all_to_all | solution.py:34
  429.4 32.7 %all-gather.24.cloned.1.call-done = f32[16384,128]{0,1:T(8,128)} async-done(((f32[512,128]{0,1:T(8,128)}), f32[16384,128]{0,1:T(8,128)}) %all-gather.24.cloned.1.call-update) | async-done | bytes 8388624 | tf_op jit(solution)/shard_map/all_gather | solution.py:39
  462.1 9.9 %copy.36 = f32[16,8,32,512]{3,2,1,0:T(8,128)S(1)} copy(f32[16,8,32,512]{3,1,2,0:T(8,128)} %bitcast.209) | data formatting | bytes 16777216
  474.2 5.5 %subtract_select_fusion = f32[512,2048]{1,0:T(8,128)} fusion(f32[512,2048]{1,0:T(8,128)S(1)} %copy-done.2, f32[512,128]{0,1:T(8,128)S(1)} %copy-done.6, pred[2048]{0:T(1024)(128)(4,1)S(1)} %fusion.23, pred[512]{0:T(512)(128)(4,1)S(1)} %fusion.25, f32[512,128]{0,1:T(8,128)S(1)} %bitcast.244, f32[512,128]{0,1:T(8,128)S(1)} %bitcast.245, ...), kind=kOutput, calls=%fused_computation | convolution fusion | flops 1614544896 | bytes 9701888 | tf_op jit(solution)/shard_map/dot_general | solution.py:90
  (100 shorter events, 45.0 us)
Async XLA Ops:
  7.2 397.6 %copy-start = (bf16[64,2048]{1,0:T(8,128)(2,1)S(1)}, bf16[64,2048]{1,0:T(8,128)(2,1)}, u32[]{:S(2)}) copy-start(bf16[64,2048]{1,0:T(8,128)(2,1)} %param.7) | copy-start | bytes 786436
  9.2 82.8 %copy-start.7 = (f32[512]{0:T(512)S(1)}, f32[512]{0:T(512)}, u32[]{:S(2)}) copy-start(f32[512]{0:T(512)} %param.8) | copy-start | bytes 6148
  9.2 38.3 %all-to-all-start = ((bf16[8,32,2048]{2,1,0:T(8,128)(2,1)}), bf16[8,32,2048]{2,1,0:T(8,128)(2,1)S(1)}, u32[]{:S(2)}, u32[]{:S(2)}) async-start(bf16[8,32,2048]{2,1,0:T(8,128)(2,1)} %broadcast_in_dim.15), calls=%async_computation | async-start | bytes 2097152 | tf_op jit(solution)/shard_map/all_to_all | solution.py:20
  18.4 73.7 %all-gather.12.cloned.1.call-start = ((), (), s32[]{:S(2)}) async-start(), calls=%async_computation.3 | async-start | bytes 4325376 | tf_op jit(solution)/shard_map/all_gather | solution.py:57
  67.4 24.6 %all-to-all-start.1 = ((bf16[32,32,512]{2,1,0:T(8,128)(2,1)}), bf16[32,32,512]{2,1,0:T(8,128)(2,1)S(1)}, u32[]{:S(2)}, u32[]{:S(2)}) async-start(bf16[32,32,512]{2,1,0:T(8,128)(2,1)} %constant_dynamic-update-slice_fusion), calls=%async_computation.1 | async-start | bytes 2097152 | tf_op jit(solution)/shard_map/all_to_all | solution.py:52
  75.0 54.2 %all-gather.18.cloned.1.call-start = ((), (), s32[]{:S(2)}) async-start(), calls=%async_computation.6 | async-start | bytes 2359296 | tf_op jit(solution)/shard_map/all_gather | solution.py:39
  97.0 2.0 copy-start.3
  99.8 84.3 %all-gather.14.cloned.1.call-start = ((), (), s32[]{:S(2)}) async-start(), calls=%async_computation.4 | async-start | bytes 2162688 | tf_op jit(solution)/shard_map/all_gather | solution.py:39
  130.7 137.5 %all-gather.20.cloned.1.call-start = ((), (), s32[]{:S(2)}) async-start(), calls=%async_computation.7 | async-start | bytes 8650752 | tf_op jit(solution)/shard_map/all_gather | solution.py:39
  210.8 112.4 %all-gather.22.cloned.1.call-start = ((), (), s32[]{:S(2)}) async-start(), calls=%async_computation.8 | async-start | bytes 2359296 | tf_op jit(solution)/shard_map/all_gather | solution.py:39
  268.2 11.2 %copy-start.5 = (f32[512,128]{0,1:T(8,128)S(1)}, f32[512,128]{0,1:T(8,128)}, u32[]{:S(2)}) copy-start(f32[512,128]{0,1:T(8,128)} %convolution_bitcast_fusion.2) | copy-start | bytes 786436
  278.1 2.2 copy-start.4
  284.4 2.0 copy-start.1
  287.2 90.8 %all-gather.16.cloned.1.call-start = ((), (), s32[]{:S(2)}) async-start(), calls=%async_computation.5 | async-start | bytes 2162688 | tf_op jit(solution)/shard_map/all_gather | solution.py:39
  324.7 137.4 %all-gather.24.cloned.1.call-start = ((), (), s32[]{:S(2)}) async-start(), calls=%async_computation.9 | async-start | bytes 8650752 | tf_op jit(solution)/shard_map/all_gather | solution.py:39
  404.7 23.7 %copy-start.6 = (f32[512,128]{0,1:T(8,128)S(1)}, f32[512,128]{0,1:T(8,128)}, u32[]{:S(2)}) copy-start(f32[512,128]{0,1:T(8,128)} %convolution_bitcast_fusion.1) | copy-start | bytes 786436
  409.1 18.6 %all-to-all-start.2 = ((f32[8,64,128]{2,1,0:T(8,128)}), f32[8,64,128]{2,1,0:T(8,128)S(1)}, u32[]{:S(2)}, u32[]{:S(2)}) async-start(f32[8,64,128]{2,1,0:T(8,128)} %bitcast.201), calls=%async_computation.2 | async-start | bytes 524288 | tf_op jit(solution)/shard_map/all_to_all | solution.py:34
  472.0 2.2 copy-start.2
Sparse Core Ops, SparseCore 0:
  21.7 53.3 all-gather.11
  99.9 29.2 all-gather.17
  132.3 51.7 all-gather.13
  211.0 57.1 all-gather.19
  287.3 35.8 all-gather.21
  326.2 51.7 all-gather.15
  404.9 57.1 all-gather.23
